TPU v7x, 32 devices: a whole 2x2x4 slice. The times are simulated.
32 devices in a mesh: space: 4 (over x, core), mem: 8 (over z, y).
Axes of the slice: x: 2, y: 2, z: 4, core: 2. Of those that a mesh axis runs over, the one named last changes fastest.
Arguments:
- prior_ensemble: float32 [512, 8192], P('mem', 'space'), may hold values from -5 to 5
- terminal_particles: float32 [512, 8192], P(None, ('space', 'mem')), may hold values from -5 to 5
- reverse_perturbation: float32 [3, 512, 8192], P(None, None, ('space', 'mem')), may hold values from -6 to 6
- measured_angles: float32 [8192], P(('space', 'mem')), may hold values from -1.3 to 1.3
Outputs:
- analysis: float32 [512, 8192], P(None, ('space', 'mem'))
All inputs are finite; a program needn't handle non-finite values.
Results may differ from a plain program's by a relative error of at most 0.0003.
Values sent between devices are 32-bit elements; how exact they have to be, the bound alone decides.
A program may use at most 64 MiB of HBM per device.

v0:
```python
import math
import jax
import jax.numpy as jnp
from jax import lax
from jax.sharding import PartitionSpec as P

ITERS = 3


def member_weights(inner_pairing_matrix, particle_lengths, alpha, sigma2, temper):
    logits = (2.0 * alpha * inner_pairing_matrix - alpha * alpha * particle_lengths[None, :]) / (
        2.0 * sigma2 * temper
    )
    return jax.nn.softmax(logits, axis=1)


def per_device(prior_ensemble, terminal_particles, reverse_perturbation, measured_angles):
    peak_log_likelihood = lax.Precision.HIGHEST
    particle_vectors = lax.all_to_all(
        prior_ensemble, "mem", split_axis=1, concat_axis=0, tiled=True
    )
    devices_all = lax.axis_size("space") * lax.axis_size("mem")
    temper = math.sqrt(particle_vectors.shape[1] * devices_all)
    local_norms = jnp.sum(prior_ensemble * prior_ensemble, axis=1)
    summed = lax.psum(local_norms, "space")
    particle_lengths = lax.all_gather(summed, "mem", axis=0, tiled=True)
    gaussian_variates = terminal_particles
    for step in range(ITERS):
        t = 1.0 - step / ITERS
        dt = 1.0 / ITERS
        alpha = 1.0 - 0.5 * t
        drift = -0.5 / alpha
        g2 = 1.0 + t / alpha
        damp = 1.0 - t
        partial_gram = jnp.einsum(
            "sv,mv->sm",
            gaussian_variates,
            particle_vectors,
            precision=peak_log_likelihood,
            preferred_element_type=jnp.float32,
        )
        inner_pairing_matrix = lax.psum(partial_gram, ("space", "mem"))
        annealed_importance = member_weights(
            inner_pairing_matrix, particle_lengths, alpha, t, temper
        )
        mixed_correction = jnp.dot(
            annealed_importance,
            particle_vectors,
            precision=peak_log_likelihood,
            preferred_element_type=jnp.float32,
        )
        score = -(gaussian_variates - alpha * mixed_correction) / t + damp * 4.0 * (
            measured_angles[None, :] - jnp.arctan(gaussian_variates)
        ) / (1.0 + gaussian_variates * gaussian_variates)
        gaussian_variates = (
            gaussian_variates
            + dt * (-drift * gaussian_variates + g2 * score)
            + math.sqrt(dt * g2) * reverse_perturbation[step]
        )
    return gaussian_variates


def solution(mesh):
    in_specs = (
        P("mem", "space"),
        P(None, ("space", "mem")),
        P(None, None, ("space", "mem")),
        P(("space", "mem")),
    )
    out_specs = P(None, ("space", "mem"))
    return jax.shard_map(
        per_device, mesh=mesh, in_specs=in_specs, out_specs=out_specs, check_vma=False
    )
```

profile of v0, /device:TPU:0, one launch (start us, length us, event | category | flops | bytes accessed | tf_op | source)
XLA Modules:
  0.0 456.9 jit_solution(2915807042031662705)
XLA Ops:
  6.5 0.0 all-reduce.5.cloned.1.call-start
  6.5 1.1 copy.8
  7.7 21.6 %all_to_all.19 = f32[64,8,256]{2,0,1:T(8,128)S(1)} all-to-all(f32[64,8,256]{2,0,1:T(8,128)S(1)} %bitcast.29), channel_id=1, replica_groups=mesh['space'=4,'mem'=8] {'mem'}, dimensions={1} | all-to-all | bytes 1048576 | tf_op jit(solution)/shard_map/all_to_all | solution.py:19
  29.3 0.0 copy-done.4
  29.3 2.1 fusion.1
  31.4 0.0 all-reduce.5.cloned.1.call-update
  31.4 0.0 copy-done
  31.4 0.0 all-reduce.7.cloned.1.call-start
  31.5 0.0 copy-done.8
  31.5 0.6 dynamic-slice
  32.7 0.1 multiply_reduce_fusion
  32.9 5.7 %psum.29 = f32[64]{0:T(128)S(1)} all-reduce(f32[64]{0:T(128)S(1)} %multiply_reduce_fusion), channel_id=1, replica_groups=mesh['space'=4,'mem'=8] {'space'}, use_global_device_ids=true, to_apply=%region_2.0 | all-reduce | flops 64 | bytes 512 | tf_op jit(solution)/shard_map/psum | solution.py:25
  38.5 0.2 dynamic-update-slice
  38.8 20.0 %all-reduce = f32[512]{0:T(512)S(1)} all-reduce(f32[512]{0:T(512)S(1)} %dynamic-update-slice), channel_id=1, replica_groups=mesh['space'=4,'mem'=8] {'mem'}, use_global_device_ids=true, to_apply=%add | all-reduce | flops 512 | bytes 4096
  58.8 102.5 %all-reduce.5.cloned.1.call-done = f32[512,512]{1,0:T(8,128)} async-done(((f32[512,512]{1,0:T(8,128)}), f32[512,512]{1,0:T(8,128)}) %all-reduce.5.cloned.1.call-update) | async-done | bytes 1048592 | tf_op jit(solution)/shard_map/psum | solution.py:42
  161.3 2.4 subtract_multiply_fusion.2
  163.7 3.7 online-softmax
  167.4 0.0 copy-done.6
  167.4 3.9 fusion
  171.3 0.0 all-reduce.7.cloned.1.call-update
  171.3 0.2 all-reduce.9.cloned.1.call-start
  171.6 129.5 %all-reduce.7.cloned.1.call-done = f32[512,512]{1,0:T(8,128)} async-done(((f32[512,512]{1,0:T(8,128)}), f32[512,512]{1,0:T(8,128)}) %all-reduce.7.cloned.1.call-update) | async-done | bytes 1048592 | tf_op jit(solution)/shard_map/psum | solution.py:42
  301.1 2.4 subtract_multiply_fusion.1
  303.5 3.6 online-softmax.1
  307.1 2.8 bitcast_add_fusion.1
  309.9 0.0 copy-done.2
  309.9 2.1 fusion.2
  312.0 0.0 all-reduce.9.cloned.1.call-update
  312.0 129.8 %all-reduce.9.cloned.1.call-done = f32[512,512]{1,0:T(8,128)} async-done(((f32[512,512]{1,0:T(8,128)}), f32[512,512]{1,0:T(8,128)}) %all-reduce.9.cloned.1.call-update) | async-done | bytes 1048592 | tf_op jit(solution)/shard_map/psum | solution.py:42
  441.8 2.4 subtract_multiply_fusion
  444.2 3.6 online-softmax.2
  447.7 2.7 bitcast_add_fusion
  (15 shorter events, 0.0 us)
Async XLA Ops:
  6.5 22.8 %copy-start.4 = (f32[512,256]{1,0:T(8,128)S(1)}, f32[512,256]{1,0:T(8,128)}, u32[]{:S(2)}) copy-start(f32[512,256]{1,0:T(8,128)} %param.5) | copy-start | bytes 1572868
  6.5 154.7 %all-reduce.5.cloned.1.call-start = ((), (), s32[]{:S(2)}) async-start(), calls=%async_computation.1 | async-start | bytes 2097152 | tf_op jit(solution)/shard_map/psum | solution.py:42
  29.3 2.1 copy-start
  29.3 2.2 copy-start.8
  29.3 3.4 copy-start.3
  31.4 269.7 %all-reduce.7.cloned.1.call-start = ((), (), s32[]{:S(2)}) async-start(), calls=%async_computation.2 | async-start | bytes 2097152 | tf_op jit(solution)/shard_map/psum | solution.py:42
  161.3 6.1 %copy-start.7 = (f32[256]{0:T(256)S(1)}, f32[256]{0:T(256)}, u32[]{:S(2)}) copy-start(f32[256]{0:T(256)} %param.7) | copy-start | bytes 3076
  163.7 3.7 copy-start.1
  163.7 3.7 copy-start.6
  171.3 270.4 %all-reduce.9.cloned.1.call-start = ((), (), s32[]{:S(2)}) async-start(), calls=%async_computation.3 | async-start | bytes 2097152 | tf_op jit(solution)/shard_map/psum | solution.py:42
  303.5 3.6 copy-start.5
  307.1 2.8 copy-start.2
Sparse Core Ops, SparseCore 0:
  31.5 129.6 all-reduce.4
  171.5 129.5 all-reduce.6
  312.1 129.6 all-reduce.8
where the time goes:
time: 457 us
  waiting for transfers between devices  362 us (79%)
  blocking collectives  47.3 us (10%)
  between operations  13.8 us (3%)
  other arithmetic  12.8 us (3%)
  Pallas kernels  10.9 us (2%)
  matrix products  8.05 us (2%)
    psum x3, waiting for transfers between devices, per_device(): inner_pairing_matrix = lax.psum(partial_gram, ('space', 'mem'))  362 us
    all_to_all x1, blocking collectives, per_device(): lax.all_to_all(prior_ensemble, 'mem', split_axis=1, concat_axis=0, tiled=...  21.6 us
    unnamed x1, blocking collectives  20 us
    unnamed x3, Pallas kernels  10.9 us
  transfers between devices with their start and end apart: 3, of which 3 were waited for; matrix products, arithmetic and copies ran while one was open for 0% of the time, Pallas kernels for 0%

commit v1 on v0

--- a/solution.py
+++ b/solution.py
@@ -39,7 +39,8 @@
             precision=peak_log_likelihood,
             preferred_element_type=jnp.float32,
         )
-        inner_pairing_matrix = lax.psum(partial_gram, ("space", "mem"))
+        terms = lax.all_gather(partial_gram, ("space", "mem"), axis=0, tiled=False)
+        inner_pairing_matrix = terms.sum(axis=0)
         annealed_importance = member_weights(
             inner_pairing_matrix, particle_lengths, alpha, t, temper
         )

time: 457 us -> 680 us (1.49)
  waiting for transfers between devices: 362 us -> 550 us
  other arithmetic: 12.8 us -> 45.9 us
    all_gather x0 -> x3, waiting for transfers between devices: none -> 550 us  [per_device(): terms = lax.all_gather(partial_gram, ('space', 'mem'), axis=0, tiled=False)]
    psum x3 -> x0, waiting for transfers between devices: 362 us -> none  [per_device(): inner_pairing_matrix = lax.psum(partial_gram, ('space', 'mem'))]
    reduce_sum x0 -> x3, other arithmetic: none -> 36.8 us  [per_device(): inner_pairing_matrix = terms.sum(axis=0)]
where the time goes in v1:
time: 680 us; the launch traced here: 679 us
  waiting for transfers between devices  550 us (81%)
  blocking collectives  48.3 us (7%)
  other arithmetic  45.9 us (7%)
  between operations  13.8 us (2%)
  Pallas kernels  10.9 us (2%)
  matrix products  7.91 us (1%)
    all_gather x3, waiting for transfers between devices, per_device(): terms = lax.all_gather(partial_gram, ('space', 'mem'), axis=0, tiled=False)  550 us
    reduce_sum x3, other arithmetic, per_device(): inner_pairing_matrix = terms.sum(axis=0)  36.8 us
    all_to_all x1, blocking collectives, per_device(): lax.all_to_all(prior_ensemble, 'mem', split_axis=1, concat_axis=0, tiled=...  21.6 us
    unnamed x1, blocking collectives  21 us
  transfers between devices with their start and end apart: 3, of which 3 were waited for; matrix products, arithmetic and copies ran while one was open for 0% of the time, Pallas kernels for 0%

profile of v1, /device:TPU:0, one launch (start us, length us, event | category | flops | bytes accessed | tf_op | source)
XLA Modules:
  0.0 679.3 jit_solution(8825237776649882494)
XLA Ops:
  6.5 1.1 copy.8
  7.7 21.6 %all_to_all.19 = f32[64,8,256]{2,0,1:T(8,128)S(1)} all-to-all(f32[64,8,256]{2,0,1:T(8,128)S(1)} %bitcast.35), channel_id=1, replica_groups=mesh['space'=4,'mem'=8] {'mem'}, dimensions={1} | all-to-all | bytes 1048576 | tf_op jit(solution)/shard_map/all_to_all | solution.py:19
  29.3 2.0 fusion.1
  31.4 0.0 all-gather.7.cloned.1.call-update
  31.4 0.0 all-gather.9.cloned.1.call-start
  31.4 0.6 dynamic-slice
  32.7 0.1 multiply_reduce_fusion
  32.8 5.7 psum.7
  38.5 0.2 dynamic-update-slice
  38.7 21.0 %all-reduce = f32[512]{0:T(512)S(1)} all-reduce(f32[512]{0:T(512)S(1)} %dynamic-update-slice), channel_id=1, replica_groups=mesh['space'=4,'mem'=8] {'mem'}, use_global_device_ids=true, to_apply=%add | all-reduce | flops 512 | bytes 4096
  59.8 165.2 %all-gather.7.cloned.1.call-done = f32[16384,512]{1,0:T(8,128)} async-done(((f32[512,512]{1,0:T(8,128)}), f32[16384,512]{1,0:T(8,128)}) %all-gather.7.cloned.1.call-update) | async-done | bytes 33554448 | tf_op jit(solution)/shard_map/all_gather | solution.py:42
  225.0 12.3 %reduce_sum.63 = f32[512,512]{1,0:T(8,128)S(1)} reduce(f32[32,512,512]{2,1,0:T(8,128)} %bitcast.25, f32[]{:T(128)} %constant.24.clone.1), dimensions={0}, to_apply=%region_0.0 | reduce | flops 8126464 | bytes 34603012 | tf_op jit(solution)/shard_map/reduce_sum | solution.py:43
  237.3 0.0 copy-start.7
  237.3 1.1 subtract_multiply_fusion.2
  238.4 3.7 online-softmax
  242.2 3.9 fusion
  246.0 0.0 all-gather.9.cloned.1.call-update
  246.1 0.2 all-gather.11.cloned.1.call-start
  246.3 192.3 %all-gather.9.cloned.1.call-done = f32[16384,512]{1,0:T(8,128)} async-done(((f32[512,512]{1,0:T(8,128)}), f32[16384,512]{1,0:T(8,128)}) %all-gather.9.cloned.1.call-update) | async-done | bytes 33554448 | tf_op jit(solution)/shard_map/all_gather | solution.py:42
  438.6 12.3 %reduce_sum.66 = f32[512,512]{1,0:T(8,128)S(1)} reduce(f32[32,512,512]{2,1,0:T(8,128)} %bitcast.26, f32[]{:T(128)} %constant.24.clone.1), dimensions={0}, to_apply=%region_5.0 | reduce | flops 8126464 | bytes 34603012 | tf_op jit(solution)/shard_map/reduce_sum | solution.py:43
  450.8 1.1 subtract_multiply_fusion.1
  452.0 3.6 online-softmax.1
  455.6 0.0 copy-done.5
  455.6 2.8 bitcast_add_fusion.1
  458.4 0.0 copy-done.2
  458.4 2.0 fusion.2
  460.4 0.0 all-gather.11.cloned.1.call-update
  460.4 192.5 %all-gather.11.cloned.1.call-done = f32[16384,512]{1,0:T(8,128)} async-done(((f32[512,512]{1,0:T(8,128)}), f32[16384,512]{1,0:T(8,128)}) %all-gather.11.cloned.1.call-update) | async-done | bytes 33554448 | tf_op jit(solution)/shard_map/all_gather | solution.py:42
  653.0 12.3 %reduce_sum.68 = f32[512,512]{1,0:T(8,128)S(1)} reduce(f32[32,512,512]{2,1,0:T(8,128)} %bitcast.27, f32[]{:T(128)} %constant.24.clone.1), dimensions={0}, to_apply=%region_8.0 | reduce | flops 8126464 | bytes 34603012 | tf_op jit(solution)/shard_map/reduce_sum | solution.py:43
  665.2 1.1 subtract_multiply_fusion
  666.4 3.6 online-softmax.2
  669.9 2.9 bitcast_add_fusion
  (18 shorter events, 0.0 us)
Async XLA Ops:
  6.5 22.8 %copy-start.4 = (f32[512,256]{1,0:T(8,128)S(1)}, f32[512,256]{1,0:T(8,128)}, u32[]{:S(2)}) copy-start(f32[512,256]{1,0:T(8,128)} %param.5) | copy-start | bytes 1572868
  6.5 218.5 %all-gather.7.cloned.1.call-start = ((), (), s32[]{:S(2)}) async-start(), calls=%async_computation.1 | async-start | bytes 34603008 | tf_op jit(solution)/shard_map/all_gather | solution.py:42
  29.3 2.1 copy-start
  29.3 2.1 copy-start.8
  29.3 3.4 copy-start.3
  31.4 407.2 %all-gather.9.cloned.1.call-start = ((), (), s32[]{:S(2)}) async-start(), calls=%async_computation.2 | async-start | bytes 34603008 | tf_op jit(solution)/shard_map/all_gather | solution.py:42
  237.3 4.8 copy-start.7
  238.4 3.7 copy-start.1
  238.4 3.7 copy-start.6
  246.1 406.9 %all-gather.11.cloned.1.call-start = ((), (), s32[]{:S(2)}) async-start(), calls=%async_computation.3 | async-start | bytes 34603008 | tf_op jit(solution)/shard_map/all_gather | solution.py:42
  452.0 3.6 copy-start.5
  455.6 2.8 copy-start.2
Sparse Core Ops, SparseCore 0:
  31.5 193.4 all-gather.6
  246.2 192.3 all-gather.8
  460.6 192.3 all-gather.10
